TPU v7x, 256 devices: a whole 4x4x8 slice. The times are simulated.
256 devices in a mesh: row: 4 (over y), col: 16 (over x, z_hi), rep: 4 (over z_lo, core).
Axes of the slice: x: 4, y: 4, z: 8 (z_hi: 4, z_lo: 2; z = z_hi * 2 + z_lo), core: 2. Of those that a mesh axis runs over, the one named last changes fastest.
Arguments:
- a_weights: bfloat16 [4, 4096, 2048], P('rep', 'row', 'col'), may hold values from 0 to 10000, as said below
- a_flags: int32 [4, 32, 16], P('rep', 'row', 'col'), may hold values 0 or 1
- b_weights: bfloat16 [4, 2048, 32768], P('rep', 'row', 'col'), may hold values from 0 to 10000, as said below
- b_flags: int32 [4, 16, 256], P('rep', 'row', 'col'), may hold values 0 or 1
- out_flags: int32 [32, 256], P('row', ('col', 'rep')), may hold values 0 or 1
Outputs:
- two_hop: bfloat16 [4096, 32768], P('row', ('col', 'rep'))
Inputs may be any that keep to these rules, and one draw needn't show every extreme that they name: `a_weights`: positive edge weights. `b_weights`: positive edge weights.
All inputs are finite; a program needn't handle non-finite values. No bound on the sum of `a_flags` or of `b_flags` or of `out_flags` on one device may be relied on, other than what follows from the above.
Results may differ from a plain program's by a relative error of at most 0.012.
Values may be sent and summed in bfloat16 or wider, within the bound.
No kernel may reach another device: no remote copies, remote signals or barrier semaphores. Data moves between devices by JAX's collectives and lax.ppermute only.
A program may use at most 64 MiB of HBM per device.

v0:
```python
import jax
import jax.numpy as jnp
from jax import lax
from jax.sharding import PartitionSpec as P


def expand(flags, width):
    return jnp.repeat(jnp.repeat(flags, width, axis=-2), width, axis=-1)


def shards(a_weights, a_flags, b_weights, b_flags, out_flags):
    width = a_weights.shape[1] // a_flags.shape[1]
    a_masked = a_weights * expand(a_flags, width).astype(jnp.bfloat16)
    b_masked = b_weights * expand(b_flags, width).astype(jnp.bfloat16)
    deg_a = 1.0 + lax.psum(jnp.sum(a_masked, axis=(0, 2), dtype=jnp.float32), ("col", "rep"))
    walk_local = (a_masked.astype(jnp.float32) / deg_a[None, :, None]).astype(jnp.bfloat16)
    walk_a = lax.all_gather(walk_local, "col", axis=2, tiled=True)
    deg_b = 1.0 + lax.psum(jnp.sum(b_masked, axis=2, dtype=jnp.float32), "col")
    walk_b = (b_masked.astype(jnp.float32) / deg_b[:, :, None]).astype(jnp.bfloat16)
    left_rows = walk_a[0]
    partial_sum = jnp.dot(
        left_rows,
        lax.all_gather(walk_b, "row", axis=1, tiled=True)[0],
        preferred_element_type=jnp.float32,
    )
    summed = lax.psum_scatter(
        partial_sum.astype(jnp.bfloat16), "rep", scatter_dimension=1, tiled=True
    ).astype(jnp.float32)
    factor = jnp.float32(b_weights.shape[2] * lax.axis_size("col"))
    return (factor * summed * expand(out_flags, width).astype(jnp.float32)).astype(jnp.bfloat16)


def solution(mesh):
    return jax.shard_map(
        shards,
        mesh=mesh,
        in_specs=(
            P("rep", "row", "col"),
            P("rep", "row", "col"),
            P("rep", "row", "col"),
            P("rep", "row", "col"),
            P("row", ("col", "rep")),
        ),
        out_specs=P("row", ("col", "rep")),
        check_vma=False,
    )
```

profile of v0, /device:TPU:1, one launch (start us, length us, event | category | flops | bytes accessed | tf_op | source)
XLA Modules:
  0.0 379.0 jit_solution(2328880365797852931)
XLA Ops:
  6.5 0.0 all-gather.3.cloned.1.call-start
  6.5 0.7 convert_bitcast_fusion.1
  7.2 0.1 broadcast_bitcast_fusion
  7.3 1.3 convert_reduce_fusion.1
  8.6 128.0 %psum.14 = f32[1024]{0:T(1024)S(1)} all-reduce(f32[1024]{0:T(1024)S(1)} %convert_reduce_fusion.1), channel_id=1, replica_groups=mesh['row'=4,'col'=16,'rep'=4] {'col','rep'}, use_global_device_ids=true, to_apply=%region_1.0 | all-reduce | flops 1024 | bytes 8192 | tf_op jit(solution)/shard_map/psum | solution.py:15
  136.6 2.0 fusion.10
  138.6 0.0 all-gather.3.cloned.1.call-update
  138.6 0.0 all-gather.5.cloned.1.call-start
  138.7 0.7 convert_bitcast_fusion
  139.4 2.3 broadcast_in_dim.20
  141.7 2.8 convert_element_type.80
  144.5 2.2 convert_reduce_fusion
  146.7 33.6 %psum.15 = f32[1,512]{1,0:T(1,128)S(1)} all-reduce(f32[1,512]{1,0:T(1,128)S(1)} %bitcast.29), channel_id=1, replica_groups=mesh['row'=4,'col'=16,'rep'=4] {'col'}, use_global_device_ids=true, to_apply=%region_3.0 | all-reduce | flops 512 | bytes 4096 | tf_op jit(solution)/shard_map/psum | solution.py:18
  180.3 3.9 %fusion.2 = bf16[1,512,2048]{2,1,0:T(8,128)(2,1)} fusion(f32[512]{0:T(512)S(1)} %bitcast.28, bf16[1,512,2048]{2,1,0:T(8,128)(2,1)} %param.7, bf16[1,512,2048]{2,1,0:T(8,128)(2,1)S(1)} %convert_element_type.80), kind=kLoop, calls=%fused_computation.4 | loop fusion | flops 4194304 | bytes 6293504 | tf_op jit(solution)/shard_map/convert_element_type | solution.py:19
  184.2 0.0 all-gather.5.cloned.1.call-update
  184.2 0.0 reduce-scatter.2.cloned.1.call-start
  184.3 36.4 %all-gather.3.cloned.1.call-done = bf16[1,1024,2048]{2,1,0:T(8,128)(2,1)} async-done(((bf16[1,1024,128]{2,1,0:T(8,128)(2,1)}), bf16[1,1024,2048]{2,1,0:T(8,128)(2,1)}) %all-gather.3.cloned.1.call-update) | async-done | bytes 4194320 | tf_op jit(solution)/shard_map/all_gather | solution.py:17
  220.6 86.0 %all-gather.5.cloned.1.call-done = bf16[1,2048,2048]{2,1,0:T(8,128)(2,1)} async-done(((bf16[1,512,2048]{2,1,0:T(8,128)(2,1)}), bf16[1,2048,2048]{2,1,0:T(8,128)(2,1)}) %all-gather.5.cloned.1.call-update) | async-done | bytes 8388624 | tf_op jit(solution)/shard_map/all_gather | solution.py:23
  306.6 13.8 %fusion.4 = bf16[1024,2048]{1,0:T(8,128)(2,1)} fusion(bf16[1,2048,2048]{2,1,0:T(8,128)(2,1)} %all-gather.5.cloned.1.call-done, bf16[1,1024,2048]{2,1,0:T(8,128)(2,1)} %all-gather.3.cloned.1.call-done), kind=kOutput, calls=%fused_computation.6 | convolution fusion | flops 8592031744 | bytes 16777216 | tf_op jit(solution)/shard_map/dot_general | solution.py:21
  320.4 0.0 copy-start.1
  320.4 0.0 reduce-scatter.2.cloned.1.call-update
  320.4 0.7 copy-done.1
  321.1 0.1 copy.6
  321.2 48.7 %reduce-scatter.2.cloned.1.call-done = bf16[1024,512]{1,0:T(8,128)(2,1)} async-done(((bf16[1024,2048]{1,0:T(8,128)(2,1)}), bf16[1024,512]{1,0:T(8,128)(2,1)}) %reduce-scatter.2.cloned.1.call-update) | async-done | bytes 1048592 | tf_op jit(solution)/shard_map/reduce_scatter | solution.py:26
  369.8 0.0 copy-start
  369.9 1.2 broadcast_in_dim.22
  371.1 0.0 copy-done
  371.1 1.4 fusion.9
  (5 shorter events, 0.1 us)
Async XLA Ops:
  6.5 214.1 %all-gather.3.cloned.1.call-start = ((), (), s32[]{:S(2)}) async-start(), calls=%async_computation.1 | async-start | bytes 4456448 | tf_op jit(solution)/shard_map/all_gather | solution.py:17
  138.6 168.0 %all-gather.5.cloned.1.call-start = ((), (), s32[]{:S(2)}) async-start(), calls=%async_computation.2 | async-start | bytes 10485760 | tf_op jit(solution)/shard_map/all_gather | solution.py:23
  184.2 185.6 %reduce-scatter.2.cloned.1.call-start = ((), (), s32[]{:S(2)}) async-start(), calls=%async_computation.3 | async-start | bytes 5242880 | tf_op jit(solution)/shard_map/reduce_scatter | solution.py:26
  320.4 0.7 copy-start.1
  369.8 1.3 copy-start
Sparse Core Ops, SparseCore 0:
  138.7 81.8 all-gather.2
  222.4 84.1 all-gather.4
  320.6 49.2 reduce-scatter.1
where the time goes:
time: 379 us
  waiting for transfers between devices  171 us (45%)
  blocking collectives  162 us (43%)
  matrix products  13.8 us (4%)
  between operations  13.1 us (3%)
  other arithmetic  12.1 us (3%)
  local copies, waits for them, and re-layouts  7.21 us (2%)
    psum x1, blocking collectives, shards(): lax.psum(jnp.sum(a_masked, axis=(0, 2), dtype=jnp.float32), ('col', 'rep'))  128 us
    all_gather x1, waiting for transfers between devices, shards(): lax.all_gather(walk_b, 'row', axis=1, tiled=True)[0]  86 us
    reduce_scatter x1, waiting for transfers between devices, shards(): lax.psum_scatter(partial_sum.astype(jnp.bfloat16), 'rep', scatter_dimensi...  48.7 us
    all_gather x1, waiting for transfers between devices, shards(): walk_a = lax.all_gather(walk_local, 'col', axis=2, tiled=True)  36.4 us
    psum x1, blocking collectives, shards(): deg_b = 1.0 + lax.psum(jnp.sum(b_masked, axis=2, dtype=jnp.float32), 'col')  33.6 us
    dot_general x1, matrix products, shards(): jnp.dot(left_rows, lax.all_gather(walk_b, 'row', axis=1, tiled=True)[0],...  13.8 us
  transfers between devices with their start and end apart: 3, of which 3 were waited for; matrix products, arithmetic and copies ran while one was open for 3% of the time, Pallas kernels for 0%

commit v1 on v0

--- a/solution.py
+++ b/solution.py
@@ -1,7 +1,16 @@
+import functools
 import jax
 import jax.numpy as jnp
 from jax import lax
 from jax.sharding import PartitionSpec as P
+
+
+def slabs_manage(tile_in, link_axis, across):
+    next_value = lax.psum(tile_in, link_axis)
+    return lax.psum(next_value, across)
+
+
+order_the_marks = functools.partial(slabs_manage, link_axis="col", across="rep")
 
 
 def expand(flags, width):
@@ -12,7 +21,7 @@
     width = a_weights.shape[1] // a_flags.shape[1]
     a_masked = a_weights * expand(a_flags, width).astype(jnp.bfloat16)
     b_masked = b_weights * expand(b_flags, width).astype(jnp.bfloat16)
-    deg_a = 1.0 + lax.psum(jnp.sum(a_masked, axis=(0, 2), dtype=jnp.float32), ("col", "rep"))
+    deg_a = 1.0 + order_the_marks(jnp.sum(a_masked, axis=(0, 2), dtype=jnp.float32))
     walk_local = (a_masked.astype(jnp.float32) / deg_a[None, :, None]).astype(jnp.bfloat16)
     walk_a = lax.all_gather(walk_local, "col", axis=2, tiled=True)
     deg_b = 1.0 + lax.psum(jnp.sum(b_masked, axis=2, dtype=jnp.float32), "col")

time: 379 us -> 307 us (0.81)
  blocking collectives: 162 us -> 54.6 us
  waiting for transfers between devices: 171 us -> 208 us
    psum x1, blocking collectives: 128 us -> 12.7 us  [slabs_manage(): return lax.psum(next_value, across)]
    all_gather x1, waiting for transfers between devices: 36.4 us -> 73.3 us  [shards(): walk_a = lax.all_gather(walk_local, 'col', axis=2, tiled=True)]
    psum x1, blocking collectives: 33.6 us -> 41.9 us  [shards(): deg_b = 1.0 + lax.psum(jnp.sum(b_masked, axis=2, dtype=jnp.float32), 'col')]
  transfers between devices with their start and end apart: 3 -> 3, of which waited for: 3 -> 3; matrix products, arithmetic and copies ran while one was open for 3% -> 1% of each run, Pallas kernels for 0% -> 0%
where the time goes in v1:
time: 307 us; the launch traced here: 306 us
  waiting for transfers between devices  208 us (68%)
  blocking collectives  54.6 us (18%)
  matrix products  13.8 us (4%)
  between operations  13.2 us (4%)
  other arithmetic  9.64 us (3%)
  local copies, waits for them, and re-layouts  7.22 us (2%)
    all_gather x1, waiting for transfers between devices, shards(): lax.all_gather(walk_b, 'row', axis=1, tiled=True)[0]  85.8 us
    all_gather x1, waiting for transfers between devices, shards(): walk_a = lax.all_gather(walk_local, 'col', axis=2, tiled=True)  73.3 us
    reduce_scatter x1, waiting for transfers between devices, shards(): lax.psum_scatter(partial_sum.astype(jnp.bfloat16), 'rep', scatter_dimensi...  48.7 us
    psum x1, blocking collectives, shards(): deg_b = 1.0 + lax.psum(jnp.sum(b_masked, axis=2, dtype=jnp.float32), 'col')  41.9 us
    dot_general x1, matrix products, shards(): jnp.dot(left_rows, lax.all_gather(walk_b, 'row', axis=1, tiled=True)[0],...  13.8 us
    psum x1, blocking collectives, slabs_manage(): return lax.psum(next_value, across)  12.7 us
  transfers between devices with their start and end apart: 3, of which 3 were waited for; matrix products, arithmetic and copies ran while one was open for 1% of the time, Pallas kernels for 0%

profile of v1, /device:TPU:1, one launch (start us, length us, event | category | flops | bytes accessed | tf_op | source)
XLA Modules:
  0.0 306.3 jit_solution(12393437691834775146)
XLA Ops:
  6.5 0.0 all-gather.3.cloned.1.call-start
  6.5 0.7 convert_bitcast_fusion
  7.2 2.3 broadcast_in_dim.20
  9.5 0.0 copy-start.3
  9.5 2.8 convert_element_type.80
  12.4 0.0 copy-done.3
  12.4 0.1 broadcast_bitcast_fusion
  12.5 0.0 copy-start
  12.5 2.3 convert_reduce_fusion
  14.7 0.0 copy-done
  14.7 0.4 convert_reduce_fusion.1
  15.1 41.9 %all-reduce = (f32[1,512]{1,0:T(1,128)S(1)}, f32[1024]{0:T(1024)S(1)}) all-reduce(f32[1,512]{1,0:T(1,128)S(1)} %bitcast.28, f32[1024]{0:T(1024)S(1)} %convert_reduce_fusion.1), channel_id=1, replica_groups=mesh['row'=4,'col'=16,'rep'=4] {'col'}, use_global_device_ids=true, to_apply=%region_4.0 | all-reduce | flops 1536 | bytes 12288 | tf_op jit(solution)/shard_map/psum | solution.py:27
  57.0 12.7 %psum.22 = f32[1024]{0:T(1024)S(1)} all-reduce(f32[1024]{0:T(1024)S(1)} %get-tuple-element.6), channel_id=1, replica_groups=mesh['row'=4,'col'=16,'rep'=4] {'rep'}, use_global_device_ids=true, to_apply=%region_2.0 | all-reduce | flops 1024 | bytes 8192 | tf_op jit(solution)/shard_map/psum | solution.py:10
  69.7 1.0 fusion.10
  70.7 0.0 all-gather.3.cloned.1.call-update
  70.7 0.0 all-gather.5.cloned.1.call-start
  70.8 3.9 %fusion.2 = bf16[1,512,2048]{2,1,0:T(8,128)(2,1)} fusion(f32[512]{0:T(512)S(1)} %bitcast.29, bf16[1,512,2048]{2,1,0:T(8,128)(2,1)} %param.7, bf16[1,512,2048]{2,1,0:T(8,128)(2,1)S(1)} %convert_element_type.80), kind=kLoop, calls=%fused_computation.4 | loop fusion | flops 4194304 | bytes 6293504 | tf_op jit(solution)/shard_map/convert_element_type | solution.py:28
  74.7 0.0 all-gather.5.cloned.1.call-update
  74.7 0.0 reduce-scatter.2.cloned.1.call-start
  74.8 73.3 %all-gather.3.cloned.1.call-done = bf16[1,1024,2048]{2,1,0:T(8,128)(2,1)} async-done(((bf16[1,1024,128]{2,1,0:T(8,128)(2,1)}), bf16[1,1024,2048]{2,1,0:T(8,128)(2,1)}) %all-gather.3.cloned.1.call-update) | async-done | bytes 4194320 | tf_op jit(solution)/shard_map/all_gather | solution.py:26
  148.0 85.8 %all-gather.5.cloned.1.call-done = bf16[1,2048,2048]{2,1,0:T(8,128)(2,1)} async-done(((bf16[1,512,2048]{2,1,0:T(8,128)(2,1)}), bf16[1,2048,2048]{2,1,0:T(8,128)(2,1)}) %all-gather.5.cloned.1.call-update) | async-done | bytes 8388624 | tf_op jit(solution)/shard_map/all_gather | solution.py:32
  233.9 13.8 %fusion.4 = bf16[1024,2048]{1,0:T(8,128)(2,1)} fusion(bf16[1,2048,2048]{2,1,0:T(8,128)(2,1)} %all-gather.5.cloned.1.call-done, bf16[1,1024,2048]{2,1,0:T(8,128)(2,1)} %all-gather.3.cloned.1.call-done), kind=kOutput, calls=%fused_computation.6 | convolution fusion | flops 8592031744 | bytes 16777216 | tf_op jit(solution)/shard_map/dot_general | solution.py:30
  247.7 0.0 copy-start.2
  247.7 0.0 reduce-scatter.2.cloned.1.call-update
  247.7 0.7 copy-done.2
  248.4 0.1 copy.6
  248.4 48.7 %reduce-scatter.2.cloned.1.call-done = bf16[1024,512]{1,0:T(8,128)(2,1)} async-done(((bf16[1024,2048]{1,0:T(8,128)(2,1)}), bf16[1024,512]{1,0:T(8,128)(2,1)}) %reduce-scatter.2.cloned.1.call-update) | async-done | bytes 1048592 | tf_op jit(solution)/shard_map/reduce_scatter | solution.py:35
  297.1 0.0 copy-start.1
  297.1 1.2 broadcast_in_dim.22
  298.4 0.0 copy-done.1
  298.4 1.4 fusion.9
  (6 shorter events, 0.1 us)
Async XLA Ops:
  6.5 141.5 %all-gather.3.cloned.1.call-start = ((), (), s32[]{:S(2)}) async-start(), calls=%async_computation.1 | async-start | bytes 4456448 | tf_op jit(solution)/shard_map/all_gather | solution.py:26
  9.5 2.8 copy-start.3
  12.5 2.3 copy-start
  70.7 163.1 %all-gather.5.cloned.1.call-start = ((), (), s32[]{:S(2)}) async-start(), calls=%async_computation.2 | async-start | bytes 10485760 | tf_op jit(solution)/shard_map/all_gather | solution.py:32
  74.7 222.4 %reduce-scatter.2.cloned.1.call-start = ((), (), s32[]{:S(2)}) async-start(), calls=%async_computation.3 | async-start | bytes 5242880 | tf_op jit(solution)/shard_map/reduce_scatter | solution.py:35
  247.7 0.7 copy-start.2
  297.1 1.3 copy-start.1
Sparse Core Ops, SparseCore 0:
  70.9 77.1 all-gather.2
  149.8 83.9 all-gather.4
  247.8 49.2 reduce-scatter.1
